TPU v7x, 256 devices: a whole 4x4x8 slice. The times are simulated.
256 devices in a mesh: blk: 128 (over x_lo, z, y, core), grp: 2 (over x_hi).
Axes of the slice: x: 4 (x_hi: 2, x_lo: 2; x = x_hi * 2 + x_lo), y: 4, z: 8, core: 2. Of those that a mesh axis runs over, the one named last changes fastest.
Arguments:
- points: float32 [32768, 4096], P(('blk', 'grp')), may hold values from -40 to 40
- cand_index: int32 [256, 128], P(('blk', 'grp')), may hold values from 0 to 127, as said below
- cand_count: int32 [256], P(('blk', 'grp')), may hold values from 32 to 128
- neighbor_ids: int32 [32768, 16], P(('blk', 'grp')), may hold values from 0 to 32767
- old_dist: float32 [32768, 16], P(('blk', 'grp')), may hold values from 0.3 to 10
Outputs:
- scaled_dist: float32 [32768, 16], P(('blk', 'grp'))
Inputs may be any that keep to these rules, and one draw needn't show every extreme that they name: `cand_index`: within each row, distinct indices of rows of the block.
All inputs are finite; a program needn't handle non-finite values.
Results may differ from a plain program's by a relative error of at most 0.0003.
Values sent between devices are 32-bit elements; how exact they have to be, the bound alone decides.
A program may use at most 128 MiB of HBM per device.

v0:
```python
import functools

import jax
import jax.numpy as jnp
from jax import lax
from jax.experimental import pallas as pl
from jax.experimental.pallas import tpu as pltpu
from jax.sharding import Mesh
from jax.sharding import PartitionSpec as P

AXES = ("xl", "z", "y", "core", "grp")
SIZES = (2, 8, 4, 2, 2)
NODES = 64
MESH = pl.DeviceIdType.MESH
HIGHEST = lax.Precision.HIGHEST
PTS = 128
D = 4096
KNN = 16
QUARTER = 1024
CHUNKS = 4
WIDTH = QUARTER // CHUNKS
FAR = 1e30
DEAD = 1e35
SUM_PHASES = ((3, 0, 4), (2,), (1,))


def sort_pairs(n):
    pairs = []
    p = 1
    while p < n:
        k = p
        while k >= 1:
            for j in range(k % p, n - k, 2 * k):
                for i in range(min(k, n - j - k)):
                    if (i + j) // (2 * p) == (i + j + k) // (2 * p):
                        pairs.append((i + j, i + j + k))
            k //= 2
        p *= 2
    return pairs


SORT16 = sort_pairs(KNN)


def sort_lists(values):
    values = list(values)
    for i, j in SORT16:
        low, high = jnp.minimum(values[i], values[j]), jnp.maximum(values[i], values[j])
        values[i], values[j] = low, high
    return values


def merge_lists(a, b):
    m = [jnp.minimum(a[i], b[KNN - 1 - i]) for i in range(KNN)]
    step = KNN // 2
    while step:
        for i in range(KNN):
            if not i & step:
                low, high = jnp.minimum(m[i], m[i + step]), jnp.maximum(m[i], m[i + step])
                m[i], m[i + step] = low, high
        step //= 2
    return m


def dot_nt(a, b):
    return lax.dot_general(
        a, b, (((1,), (1,)), ((), ())), precision=HIGHEST, preferred_element_type=jnp.float32
    )


def to_lanes(block):
    wide = jnp.concatenate([block, jnp.zeros((PTS, PTS - KNN), block.dtype)], axis=1)
    return wide.T[:KNN]


def device_of(node, core, grp):
    return (node // 32, (node // 4) % 8, node % 4, core, grp)


def kernel(
    pts, cidx, ccnt, nbr, old, out,
    both, xr, fb, gx, gf, gb, gx_r, gf_r, gb_r, hx, hf, hb, rx, rv, rbv, ru,
    info, bias, tiles, nb_v, old_v, ci_v, nb_t, sum_src, sum_in,
    loc_sem, cc_v, sib_s, sib_r, x_s, x_r, yo_s, yr_s, f_r, info_s, info_r, red_s, red_r,
    t_s, rx_sem, rv_sem, rbv_sem, ru_sem, sum_s, sum_r,
):
    d = tuple(lax.axis_index(a) for a in AXES)
    c, g = d[3], d[4]
    q = d[0] * 32 + d[1] * 4 + d[2]
    up, down = (q + 1) % NODES, (q + NODES - 1) % NODES
    ahead = (q + NODES + 2 * c - 1) % NODES
    behind = (q + NODES + 1 - 2 * c) % NODES
    sibling = device_of(q, 1 - c, g)

    def remote(src, dst, send, recv, to):
        return pltpu.make_async_remote_copy(
            src_ref=src, dst_ref=dst, send_sem=send, recv_sem=recv, device_id=to, device_id_type=MESH
        )

    barrier = pltpu.get_barrier_semaphore()
    peers = [device_of(n, k, h) for n in (up, down) for k in (0, 1) for h in (0, 1)]
    sum_peers = []
    for axes in SUM_PHASES:
        count = 1
        for a in axes:
            count *= SIZES[a]
        row = []
        for offset in range(1, count):
            at, rest = list(d), offset
            for a in axes:
                at[a] = (d[a] + rest % SIZES[a]) % SIZES[a]
                rest //= SIZES[a]
            row.append(tuple(at))
        sum_peers.append(row)
        peers += row
    for peer in peers:
        pl.semaphore_signal(barrier, inc=1, device_id=peer, device_id_type=MESH)
    loads = [
        pltpu.make_async_copy(pts, both.at[c], loc_sem.at[0]),
        pltpu.make_async_copy(cidx, ci_v, loc_sem.at[1]),
        pltpu.make_async_copy(nbr, nb_v, loc_sem.at[2]),
        pltpu.make_async_copy(old, old_v, loc_sem.at[3]),
        pltpu.make_async_copy(ccnt, cc_v, loc_sem.at[4]),
    ]
    for load in loads:
        load.start()
    pl.semaphore_wait(barrier, len(peers))

    def cols(quarter, j):
        return pl.ds(pl.multiple_of(quarter * QUARTER + j * WIDTH, 128), WIDTH)

    def part(j):
        return pl.ds(j * WIDTH, WIDTH)

    def x_copy(k, j):
        return remote(
            pts.at[:, cols(2 * (1 - g) + k, j)], xr.at[c, :, part(j)], x_s.at[k, j], x_r.at[c, j],
            device_of(q, k, 1 - g),
        )

    def yo_copy(k, j):
        return remote(
            pts.at[:, cols(2 * g + k, j)], fb.at[c, g, :, part(j)], yo_s.at[k, j], f_r.at[c, g, j],
            device_of(ahead, k, g),
        )

    def sib_copy(i):
        quarter = pl.ds(pl.multiple_of(((2 * g + 1 - c + i) % 4) * QUARTER, 128), QUARTER)
        return remote(pts.at[:, quarter], both.at[c, :, quarter], sib_s.at[i], sib_r.at[i], sibling)

    def relay(way, j):
        to = device_of(up if way else down, c, g)
        return remote(
            xr.at[way, :, part(j)], fb.at[way, 1 - g, :, part(j)], yr_s.at[way, j], f_r.at[way, 1 - g, j], to
        )

    for j in range(CHUNKS):
        for k in (0, 1):
            x_copy(k, j).start()
            yo_copy(k, j).start()
        sib_copy(j).start()

    loads[1].wait()
    loads[4].wait()
    slot = lax.broadcasted_iota(jnp.int32, (PTS, PTS), 1)
    row = lax.broadcasted_iota(jnp.int32, (PTS, PTS), 0)
    hit = (jnp.broadcast_to(ci_v[...], (PTS, PTS)) == row) & (slot < cc_v[0])
    live = jnp.max(jnp.where(hit, 1.0, 0.0).T, axis=0, keepdims=True)
    loads[0].wait()
    square = jnp.zeros((PTS, PTS), jnp.float32)
    for i in range(D // PTS):
        x = both[c, :, i * PTS : (i + 1) * PTS]
        square = square + x * x
    norm = jnp.sum(square.T, axis=0, keepdims=True)
    info[0] = jnp.broadcast_to(jnp.where(live > 0.5, norm, DEAD), (8, PTS))
    info_to = [(sibling, 1)]
    info_to += [(device_of(q, k, 1 - g), 2 + c) for k in (0, 1)]
    info_to += [(device_of(ahead, k, h), 6 - 2 * c + g) for k in (0, 1) for h in (0, 1)]
    info_to += [(device_of(behind, c, h), 8 + g) for h in (0, 1)]
    info_sends = [
        remote(info.at[0], info.at[s], info_s.at[i], info_r.at[s], to) for i, (to, s) in enumerate(info_to)
    ]
    for send in info_sends:
        send.start()
    loads[2].wait()
    loads[3].wait()
    nb_t[...] = to_lanes(nb_v[...].astype(jnp.float32)).astype(jnp.int32)
    old_t = to_lanes(old_v[...])

    def block_of(s):
        odd = s % 2
        far_pair = jnp.where(s < 8, 4 * up + odd, 4 * ahead + 2 * c + odd)
        far_pair = jnp.where(s < 6, 4 * down + 2 + odd, far_pair)
        near = jnp.where(s == 0, 4 * q + 2 * c + g, 4 * q + 2 * (1 - c) + g)
        near = jnp.where(s < 2, near, 4 * q + 2 * odd + 1 - g)
        return jnp.where(s < 4, near, far_pair)

    def set_bias(s):
        first = block_of(s) * PTS
        ids = first + lax.broadcasted_iota(jnp.int32, (PTS, PTS), 0)
        own_ids = (4 * q + 2 * c + g) * PTS + lax.broadcasted_iota(jnp.int32, (PTS, PTS), 1)
        masked = ids == own_ids
        for k in range(KNN):
            masked = masked | (ids == nb_t[k : k + 1, :])
        key = jnp.broadcast_to(info[s, 0:1, :], (PTS, PTS)).T
        bias[s] = jnp.where(masked, DEAD, key + norm)

    set_bias(0)
    for ref in (gx, gf, gb):
        ref[...] = jnp.zeros_like(ref)
    tiles[0] = jnp.zeros((PTS, PTS), jnp.float32)
    tiles[1] = jnp.zeros((PTS, PTS), jnp.float32)

    def near_blocks(core, j):
        return jnp.concatenate([both[core, :, cols(2 * g + c, j)], xr[core, :, part(j)]], axis=0)

    def far_products(j):
        for way in (0, 1):
            for h in (0, 1):
                remote(
                    xr.at[way, :, part(j)], fb.at[way, h, :, part(j)], yr_s.at[way, j], f_r.at[way, h, j], sibling
                ).wait_recv()
        v0 = near_blocks(0, j)
        f = fb[1, :, :, part(j)].reshape(2 * PTS, WIDTH)
        gf[0] += dot_nt(f, v0)
        b = fb[0, :, :, part(j)].reshape(2 * PTS, WIDTH)
        gb[...] += dot_nt(b, v0)
        gf[1] += dot_nt(f, near_blocks(1, j))

    def far_quarter(j):
        sib_copy(j).wait_recv()
        quarter = pl.ds(pl.multiple_of(((2 * g + c + j) % 4) * QUARTER, 128), QUARTER)
        mine = both[c, :, quarter]
        tiles[0] += dot_nt(mine, mine)
        tiles[1] += dot_nt(both[1 - c, :, quarter], mine)

    gx_copy = remote(gx, gx_r, red_s.at[0], red_r.at[0], sibling)
    gf_copy = remote(gf.at[1 - c], gf_r, red_s.at[1], red_r.at[1], sibling)
    gb_copy = remote(gb, gb_r, red_s.at[2], red_r.at[2], sibling)

    for j in range(CHUNKS):
        for way in (0, 1):
            remote(
                pts.at[:, cols(0, 0)], xr.at[way, :, part(j)], x_s.at[0, j], x_r.at[way, j], sibling
            ).wait_recv()
            relay(way, j).start()
        far_quarter(j)
        xs = jnp.concatenate([xr[0, :, part(j)], xr[1, :, part(j)]], axis=0)
        own = jnp.concatenate([both[0, :, cols(2 * g + c, j)], both[1, :, cols(2 * g + c, j)]], axis=0)
        gx[...] += dot_nt(xs, own)
        if j == 0:

            def each(s, carry):
                remote(info.at[0], info.at[s], info_s.at[0], info_r.at[s], sibling).wait_recv()
                set_bias(s)
                return carry

            lax.fori_loop(1, 10, each, 0)
        if j == CHUNKS - 1:
            gx_copy.start()
        if j > 0:
            far_products(j - 1)

    gx_copy.wait_recv()
    total = gx[...] + gx_r[...]
    for k in (0, 1):
        hx[k] = total[k * PTS : (k + 1) * PTS]
    other = device_of(q, c, 1 - g)
    rx_copy = remote(hx.at[c], rx, t_s.at[0], rx_sem, other)
    rx_copy.start()

    far_products(CHUNKS - 1)
    gf_copy.start()

    @pl.when(c == 1)
    def _():
        gb_copy.start()

    gf_copy.wait_recv()
    total = gf[c] + gf_r[...]
    for rel in (0, 1):
        hf[rel] = total[:, rel * PTS : (rel + 1) * PTS]
    rv_copy = remote(hf.at[1], rv, t_s.at[1], rv_sem, other)
    rv_copy.start()

    def ru_copy(src, half_slot, rel, h, sem, to):
        name = g if rel == 0 else 1 - g
        return remote(
            src.at[rel, pl.ds(h * PTS, PTS)], ru.at[g, half_slot, name], sem, ru_sem.at[g, half_slot, name], to
        )

    fu_copies = [
        ru_copy(hf, c, rel, h, t_s.at[2 + 2 * rel + h], device_of(down, 1, h)) for rel in (0, 1) for h in (0, 1)
    ]
    for copy in fu_copies:
        copy.start()
    rbv_copy = remote(hb.at[1], rbv, t_s.at[6], rbv_sem, device_of(q, 0, 1 - g))
    bu_copies = [
        ru_copy(hb, 1, rel, h, t_s.at[7 + 2 * rel + h], device_of(up, 0, h)) for rel in (0, 1) for h in (0, 1)
    ]

    @pl.when(c == 0)
    def _():
        gb_copy.wait_recv()
        for rel in (0, 1):
            half = pl.ds(rel * PTS, PTS)
            hb[rel] = gb[:, half] + gb_r[:, half]
        rbv_copy.start()
        for copy in bu_copies:
            copy.start()

    def taken(best, s, inner):
        value = bias[s]
        dist = jnp.where(value >= 1e34, FAR, (value - 2.0 * inner) / D)
        return merge_lists(best, sort_lists([dist[8 * i : 8 * i + 8] for i in range(KNN)]))

    low, high = jnp.minimum(old_t[:8], old_t[8:]), jnp.maximum(old_t[:8], old_t[8:])
    best = [low, high] + [jnp.full((8, PTS), FAR, jnp.float32)] * (KNN - 2)
    best = taken(best, 0, tiles[0])
    best = taken(best, 1, tiles[1])
    rx_copy.wait_recv()
    lanes = pl.ds(pl.multiple_of(c * PTS, PTS), PTS)
    for k in (0, 1):
        best = taken(best, 2 + k, hx[k, :, lanes] + rx[:, k * PTS : (k + 1) * PTS].T)
    rv_copy.wait_recv()
    for h in (0, 1):
        best = taken(best, 4 + h, hf[0, h * PTS : (h + 1) * PTS] + rv[h * PTS : (h + 1) * PTS])

    def wait_ru(half_slot):
        for half in (0, 1):
            for name in (0, 1):
                remote(
                    hf.at[0, pl.ds(0, PTS)], ru.at[half, half_slot, name], t_s.at[2], ru_sem.at[half, half_slot, name],
                    sibling,
                ).wait_recv()

    @pl.when(c == 0)
    def _():
        rbv_copy.wait_recv()
        for h in (0, 1):
            tiles[2 + h] = hb[0, h * PTS : (h + 1) * PTS] + rbv[h * PTS : (h + 1) * PTS]

    @pl.when(c == 1)
    def _():
        wait_ru(0)
        for h in (0, 1):
            tiles[2 + h] = (ru[0, 0, h] + ru[1, 0, h]).T

    for h in (0, 1):
        best = taken(best, 6 + h, tiles[2 + h])
    wait_ru(1)
    for h in (0, 1):
        best = taken(best, 8 + h, (ru[0, 1, h] + ru[1, 1, h]).T)
    for shift in (4, 2, 1):
        best = merge_lists(best, [pltpu.roll(v, shift, 0) for v in best])

    running = best[KNN - 1]
    first = 0
    for phase, row_peers in enumerate(sum_peers):
        sum_src[phase] = running
        copies = [
            remote(sum_src.at[phase], sum_in.at[first + i], sum_s.at[first + i], sum_r.at[first + i], peer)
            for i, peer in enumerate(row_peers)
        ]
        for copy in copies:
            copy.start()
        for copy in copies:
            copy.wait_recv()
        for i in range(len(copies)):
            running = running + sum_in[first + i]
        for copy in copies:
            copy.wait_send()
        first += len(copies)
    mean = jnp.sum(running[0:1, :], axis=1, keepdims=True) / (PTS * NODES * 4)
    for k in range(KNN):
        out[k : k + 1, :] = best[k][0:1, :] / mean

    for j in range(CHUNKS):
        for k in (0, 1):
            x_copy(k, j).wait_send()
            yo_copy(k, j).wait_send()
            relay(k, j).wait_send()
        sib_copy(j).wait_send()
    for send in info_sends:
        send.wait_send()
    for copy in [gx_copy, gf_copy, rx_copy, rv_copy, *fu_copies]:
        copy.wait_send()

    @pl.when(c == 1)
    def _():
        gb_copy.wait_send()

    @pl.when(c == 0)
    def _():
        rbv_copy.wait_send()
        for copy in bu_copies:
            copy.wait_send()


def body(points, cand_index, cand_count, neighbor_ids, old_dist):
    f32, dma = jnp.float32, pltpu.SemaphoreType.DMA
    n_sum = sum(len(row) for row in ([0] * 7, [0] * 3, [0] * 7))
    vmem = pltpu.VMEM
    any_spec = pl.BlockSpec(memory_space=pl.ANY)
    scratch = [
        vmem((2, PTS, D), f32),
        vmem((2, PTS, QUARTER), f32),
        vmem((2, 2, PTS, QUARTER), f32),
        vmem((256, 256), f32),
        vmem((2, 256, 256), f32),
        vmem((256, 256), f32),
        vmem((256, 256), f32),
        vmem((256, 256), f32),
        vmem((256, 256), f32),
        vmem((2, 128, 256), f32),
        vmem((2, 256, 128), f32),
        vmem((2, 256, 128), f32),
        vmem((128, 256), f32),
        vmem((256, 128), f32),
        vmem((256, 128), f32),
        vmem((2, 2, 2, 128, 128), f32),
        vmem((10, 8, 128), f32),
        vmem((10, 128, 128), f32),
        vmem((4, 128, 128), f32),
        vmem((128, 16), jnp.int32),
        vmem((128, 16), f32),
        vmem((1, 128), jnp.int32),
        vmem((16, 128), jnp.int32),
        vmem((3, 8, 128), f32),
        vmem((n_sum, 8, 128), f32),
        dma((5,)),
        pltpu.SMEM((1,), jnp.int32),
        dma((CHUNKS,)),
        dma((CHUNKS,)),
        dma((2, CHUNKS)),
        dma((2, CHUNKS)),
        dma((2, CHUNKS)),
        dma((2, CHUNKS)),
        dma((2, 2, CHUNKS)),
        dma((9,)),
        dma((10,)),
        dma((3,)),
        dma((3,)),
        dma((11,)),
        dma,
        dma,
        dma,
        dma((2, 2, 2)),
        dma((n_sum,)),
        dma((n_sum,)),
    ]
    best = pl.pallas_call(
        kernel,
        out_shape=jax.ShapeDtypeStruct((KNN, PTS), f32),
        in_specs=[any_spec] * 5,
        out_specs=pl.BlockSpec(memory_space=pltpu.VMEM),
        scratch_shapes=scratch,
        compiler_params=pltpu.CompilerParams(
            collective_id=0, has_side_effects=True, vmem_limit_bytes=40 << 20
        ),
    )(points, cand_index, cand_count, neighbor_ids, old_dist)
    return best.T


def solution(mesh):
    finer = Mesh(mesh.devices.reshape(*SIZES), AXES)
    return jax.shard_map(
        body,
        mesh=finer,
        in_specs=(P(AXES, None), P(AXES, None), P(AXES), P(AXES, None), P(AXES, None)),
        out_specs=P(AXES, None),
        check_vma=False,
    )
```

profile of v0, /device:TPU:1, one launch (start us, length us, event | category | flops | bytes accessed | tf_op | source)
XLA Modules:
  0.0 100.0 jit_solution(15378570746146693834)
XLA Ops:
  0.7 0.8 copy.6.nbr
  1.4 0.8 copy.7.old
  2.2 0.0 copy-start
  2.3 1.6 %copy-done = f32[128,4096]{1,0:T(8,128)S(1)} copy-done((f32[128,4096]{1,0:T(8,128)S(1)}, f32[128,4096]{1,0:T(8,128)}, u32[]{:S(2)}) %copy-start) | copy-done | bytes 2097176
  3.8 0.0 copy-start.1
  3.8 0.7 copy-done.1
  4.5 94.9 %shard_map.55 = f32[16,128]{1,0:T(8,128)S(1)} custom-call(f32[128,4096]{1,0:T(8,128)S(1)} %copy-done, s32[1,128]{1,0:T(1,128)S(1)} %copy-done.1, s32[1]{0:T(128)S(6)} %copy.9.ccnt, s32[128,16]{1,0:T(8,128)S(1)} %copy.6.nbr, f32[128,16]{1,0:T(8,128)S(1)} %copy.7.old), custom_call_target="tpu_custom_call" | custom-call | tf_op jit(solution)/shard_map/pallas_call | solution.py:452
  99.4 0.6 copy.10
Async XLA Ops:
  2.2 1.6 %copy-start = (f32[128,4096]{1,0:T(8,128)S(1)}, f32[128,4096]{1,0:T(8,128)}, u32[]{:S(2)}) copy-start(f32[128,4096]{1,0:T(8,128)} %pts.1) | copy-start | bytes 6291460
  3.8 0.7 copy-start.1
where the time goes:
time: 100 us
  Pallas kernels  94.9 us (95%)
  local copies, waits for them, and re-layouts  4.43 us (4%)
    pallas_call x1, Pallas kernels, body(): pl.pallas_call(kernel, out_shape=jax.ShapeDtypeStruct((KNN, PTS), f32), i...  94.9 us
    unnamed x7, local copies, waits for them, and re-layouts  4.43 us

commit v1 on v0

--- a/solution.py
+++ b/solution.py
@@ -21,7 +21,7 @@
 WIDTH = QUARTER // CHUNKS
 FAR = 1e30
 DEAD = 1e35
-SUM_PHASES = ((3, 0, 4), (2,), (1,))
+SUM_PHASES = ((3,), (0, 4, 2), (1,))
 
 
 def sort_pairs(n):
@@ -66,11 +66,6 @@
     return lax.dot_general(
         a, b, (((1,), (1,)), ((), ())), precision=HIGHEST, preferred_element_type=jnp.float32
     )
-
-
-def to_lanes(block):
-    wide = jnp.concatenate([block, jnp.zeros((PTS, PTS - KNN), block.dtype)], axis=1)
-    return wide.T[:KNN]
 
 
 def device_of(node, core, grp):
@@ -91,6 +86,18 @@
     ahead = (q + NODES + 2 * c - 1) % NODES
     behind = (q + NODES + 1 - 2 * c) % NODES
     sibling = device_of(q, 1 - c, g)
+    turned = d[0]
+
+    def turn(bit, by):
+        return bit + by - 2 * bit * by
+
+    def quarter_at(core, grp):
+        return 2 * turn(grp, core * turned) + core
+
+    def same_quarter(node, core, grp):
+        return device_of(node, core, turn(grp, core * turn(turned, node // 32)))
+
+    mine_at = quarter_at(c, g)
 
     def remote(src, dst, send, recv, to):
         return pltpu.make_async_remote_copy(
@@ -99,6 +106,7 @@
 
     barrier = pltpu.get_barrier_semaphore()
     peers = [device_of(n, k, h) for n in (up, down) for k in (0, 1) for h in (0, 1)]
+    peers.append(device_of(q, 1 - c, 1 - g))
     sum_peers = []
     for axes in SUM_PHASES:
         count = 1
@@ -134,22 +142,22 @@
 
     def x_copy(k, j):
         return remote(
-            pts.at[:, cols(2 * (1 - g) + k, j)], xr.at[c, :, part(j)], x_s.at[k, j], x_r.at[c, j],
+            pts.at[:, cols(quarter_at(k, 1 - g), j)], xr.at[c, :, part(j)], x_s.at[k, j], x_r.at[c, j],
             device_of(q, k, 1 - g),
         )
 
     def yo_copy(k, j):
         return remote(
-            pts.at[:, cols(2 * g + k, j)], fb.at[c, g, :, part(j)], yo_s.at[k, j], f_r.at[c, g, j],
-            device_of(ahead, k, g),
+            pts.at[:, cols(quarter_at(k, g), j)], fb.at[c, g, :, part(j)], yo_s.at[k, j], f_r.at[c, g, j],
+            same_quarter(ahead, k, g),
         )
 
     def sib_copy(i):
-        quarter = pl.ds(pl.multiple_of(((2 * g + 1 - c + i) % 4) * QUARTER, 128), QUARTER)
+        quarter = pl.ds(pl.multiple_of(((quarter_at(1 - c, g) + i) % 4) * QUARTER, 128), QUARTER)
         return remote(pts.at[:, quarter], both.at[c, :, quarter], sib_s.at[i], sib_r.at[i], sibling)
 
     def relay(way, j):
-        to = device_of(up if way else down, c, g)
+        to = same_quarter(up if way else down, c, g)
         return remote(
             xr.at[way, :, part(j)], fb.at[way, 1 - g, :, part(j)], yr_s.at[way, j], f_r.at[way, 1 - g, j], to
         )
@@ -184,8 +192,8 @@
         send.start()
     loads[2].wait()
     loads[3].wait()
-    nb_t[...] = to_lanes(nb_v[...].astype(jnp.float32)).astype(jnp.int32)
-    old_t = to_lanes(old_v[...])
+    nb_t[...] = nb_v[...]
+    old_t = old_v[...]
 
     def block_of(s):
         odd = s % 2
@@ -212,7 +220,7 @@
     tiles[1] = jnp.zeros((PTS, PTS), jnp.float32)
 
     def near_blocks(core, j):
-        return jnp.concatenate([both[core, :, cols(2 * g + c, j)], xr[core, :, part(j)]], axis=0)
+        return jnp.concatenate([both[core, :, cols(mine_at, j)], xr[core, :, part(j)]], axis=0)
 
     def far_products(j):
         for way in (0, 1):
@@ -229,7 +237,7 @@
 
     def far_quarter(j):
         sib_copy(j).wait_recv()
-        quarter = pl.ds(pl.multiple_of(((2 * g + c + j) % 4) * QUARTER, 128), QUARTER)
+        quarter = pl.ds(pl.multiple_of(((mine_at + j) % 4) * QUARTER, 128), QUARTER)
         mine = both[c, :, quarter]
         tiles[0] += dot_nt(mine, mine)
         tiles[1] += dot_nt(both[1 - c, :, quarter], mine)
@@ -246,16 +254,8 @@
             relay(way, j).start()
         far_quarter(j)
         xs = jnp.concatenate([xr[0, :, part(j)], xr[1, :, part(j)]], axis=0)
-        own = jnp.concatenate([both[0, :, cols(2 * g + c, j)], both[1, :, cols(2 * g + c, j)]], axis=0)
+        own = jnp.concatenate([both[0, :, cols(mine_at, j)], both[1, :, cols(mine_at, j)]], axis=0)
         gx[...] += dot_nt(xs, own)
-        if j == 0:
-
-            def each(s, carry):
-                remote(info.at[0], info.at[s], info_s.at[0], info_r.at[s], sibling).wait_recv()
-                set_bias(s)
-                return carry
-
-            lax.fori_loop(1, 10, each, 0)
         if j == CHUNKS - 1:
             gx_copy.start()
         if j > 0:
@@ -269,6 +269,12 @@
     rx_copy = remote(hx.at[c], rx, t_s.at[0], rx_sem, other)
     rx_copy.start()
 
+    def each(s, carry):
+        remote(info.at[0], info.at[s], info_s.at[0], info_r.at[s], sibling).wait_recv()
+        set_bias(s)
+        return carry
+
+    lax.fori_loop(1, 10, each, 0)
     far_products(CHUNKS - 1)
     gf_copy.start()
 
@@ -354,7 +360,8 @@
     for shift in (4, 2, 1):
         best = merge_lists(best, [pltpu.roll(v, shift, 0) for v in best])
 
-    running = best[KNN - 1]
+    running = best[KNN - 1][0:1, :]
+    sum_copies = []
     first = 0
     for phase, row_peers in enumerate(sum_peers):
         sum_src[phase] = running
@@ -368,10 +375,9 @@
             copy.wait_recv()
         for i in range(len(copies)):
             running = running + sum_in[first + i]
-        for copy in copies:
-            copy.wait_send()
+        sum_copies += copies
         first += len(copies)
-    mean = jnp.sum(running[0:1, :], axis=1, keepdims=True) / (PTS * NODES * 4)
+    mean = jnp.sum(running, axis=1, keepdims=True) / (PTS * NODES * 4)
     for k in range(KNN):
         out[k : k + 1, :] = best[k][0:1, :] / mean
 
@@ -383,7 +389,7 @@
         sib_copy(j).wait_send()
     for send in info_sends:
         send.wait_send()
-    for copy in [gx_copy, gf_copy, rx_copy, rv_copy, *fu_copies]:
+    for copy in [gx_copy, gf_copy, rx_copy, rv_copy, *fu_copies, *sum_copies]:
         copy.wait_send()
 
     @pl.when(c == 1)
@@ -399,9 +405,9 @@
 
 def body(points, cand_index, cand_count, neighbor_ids, old_dist):
     f32, dma = jnp.float32, pltpu.SemaphoreType.DMA
-    n_sum = sum(len(row) for row in ([0] * 7, [0] * 3, [0] * 7))
+    n_sum = 1 + 15 + 7
     vmem = pltpu.VMEM
-    any_spec = pl.BlockSpec(memory_space=pl.ANY)
+    any_spec = pl.BlockSpec(memory_space=pltpu.HBM)
     scratch = [
         vmem((2, PTS, D), f32),
         vmem((2, PTS, QUARTER), f32),
@@ -422,12 +428,12 @@
         vmem((10, 8, 128), f32),
         vmem((10, 128, 128), f32),
         vmem((4, 128, 128), f32),
-        vmem((128, 16), jnp.int32),
-        vmem((128, 16), f32),
+        vmem((16, 128), jnp.int32),
+        vmem((16, 128), f32),
         vmem((1, 128), jnp.int32),
         vmem((16, 128), jnp.int32),
-        vmem((3, 8, 128), f32),
-        vmem((n_sum, 8, 128), f32),
+        vmem((3, 1, 128), f32),
+        vmem((n_sum, 1, 128), f32),
         dma((5,)),
         pltpu.SMEM((1,), jnp.int32),
         dma((CHUNKS,)),
@@ -458,7 +464,7 @@
         compiler_params=pltpu.CompilerParams(
             collective_id=0, has_side_effects=True, vmem_limit_bytes=40 << 20
         ),
-    )(points, cand_index, cand_count, neighbor_ids, old_dist)
+    )(points, cand_index, cand_count, neighbor_ids.T, old_dist.T)
     return best.T
 
 

time: 100 us -> 85.2 us (0.85)
  Pallas kernels: 94.9 us -> 79.8 us
    pallas_call x1, Pallas kernels: 94.9 us -> 79.8 us  [body(): pl.pallas_call(kernel, out_shape=jax.ShapeDtypeStruct((KNN, PTS), f32), i...]
    unnamed x7 -> x9, local copies, waits for them, and re-layouts: 4.43 us -> 4.23 us
where the time goes in v1:
time: 85.2 us; the launch traced here: 84.7 us
  Pallas kernels  79.8 us (94%)
  local copies, waits for them, and re-layouts  4.23 us (5%)
    pallas_call x1, Pallas kernels, body(): pl.pallas_call(kernel, out_shape=jax.ShapeDtypeStruct((KNN, PTS), f32), i...  79.8 us
    unnamed x9, local copies, waits for them, and re-layouts  4.23 us

profile of v1, /device:TPU:1, one launch (start us, length us, event | category | flops | bytes accessed | tf_op | source)
XLA Modules:
  0.0 84.7 jit_solution(10177153614662066417)
XLA Ops:
  0.7 0.0 copy-start
  0.7 1.6 %copy-done = f32[128,4096]{1,0:T(8,128)S(1)} copy-done((f32[128,4096]{1,0:T(8,128)S(1)}, f32[128,4096]{1,0:T(8,128)}, u32[]{:S(2)}) %copy-start) | copy-done | bytes 2097176
  2.2 0.0 copy-start.1
  2.2 0.7 copy-done.1
  2.9 0.0 copy-start.2
  2.9 0.7 copy-done.2
  3.6 0.0 copy-start.3
  3.6 0.7 copy-done.3
  4.3 79.8 %shard_map.55 = f32[16,128]{1,0:T(8,128)S(1)} custom-call(f32[128,4096]{1,0:T(8,128)S(1)} %copy-done, s32[1,128]{1,0:T(1,128)S(1)} %copy-done.3, s32[1]{0:T(128)S(6)} %copy.7.ccnt, s32[16,128]{1,0:T(8,128)S(1)} %bitcast.4, f32[16,128]{1,0:T(8,128)S(1)} %bitcast.5), custom_call_target="tpu_custom_call" | custom-call | tf_op jit(solution)/shard_map/pallas_call | solution.py:458
  84.1 0.6 copy.8
Async XLA Ops:
  0.7 1.6 %copy-start = (f32[128,4096]{1,0:T(8,128)S(1)}, f32[128,4096]{1,0:T(8,128)}, u32[]{:S(2)}) copy-start(f32[128,4096]{1,0:T(8,128)} %pts.1) | copy-start | bytes 6291460
  2.2 0.7 copy-start.1
  2.9 0.7 copy-start.2
  3.6 0.7 copy-start.3

commit v2 on v1

--- a/solution.py
+++ b/solution.py
@@ -77,7 +77,7 @@
     both, xr, fb, gx, gf, gb, gx_r, gf_r, gb_r, hx, hf, hb, rx, rv, rbv, ru,
     info, bias, tiles, nb_v, old_v, ci_v, nb_t, sum_src, sum_in,
     loc_sem, cc_v, sib_s, sib_r, x_s, x_r, yo_s, yr_s, f_r, info_s, info_r, red_s, red_r,
-    t_s, rx_sem, rv_sem, rbv_sem, ru_sem, sum_s, sum_r,
+    via, via_s, via_r, t_s, rx_sem, rv_sem, rbv_sem, ru_sem, sum_s, sum_r,
 ):
     d = tuple(lax.axis_index(a) for a in AXES)
     c, g = d[3], d[4]
@@ -121,8 +121,38 @@
             row.append(tuple(at))
         sum_peers.append(row)
         peers += row
+    ring = q % 32
+    steps = ((c == 1) & (ring == 31)) | ((c == 0) & (ring == 0))
+    passes = (ring == 28) | (ring == 3)
+    receives = (ring == 0) | (ring == 31)
+    onward = ring // 28
+    middle = q + 3 - 6 * c
+    source = device_of(q - 3 + 6 * onward, onward, g)
+    after_node = (1 - d[0]) * 32 + 31 * (1 - onward)
+    before_node = (1 - d[0]) * 32 + jnp.where(ring == 0, 28, 3)
+    onward_to = same_quarter(after_node, c, g)
+
+    def greet(peer):
+        pl.semaphore_signal(barrier, inc=1, device_id=peer, device_id_type=MESH)
+
     for peer in peers:
-        pl.semaphore_signal(barrier, inc=1, device_id=peer, device_id_type=MESH)
+        greet(peer)
+
+    @pl.when(steps)
+    def _():
+        for k in (0, 1):
+            greet(device_of(middle, k, g))
+
+    @pl.when(passes)
+    def _():
+        greet(source)
+        greet(onward_to)
+
+    @pl.when(receives)
+    def _():
+        greet(same_quarter(before_node, c, g))
+
+    greeted = len(peers) + jnp.where(steps, 2, 0) + jnp.where(passes, 2, 0) + jnp.where(receives, 1, 0)
     loads = [
         pltpu.make_async_copy(pts, both.at[c], loc_sem.at[0]),
         pltpu.make_async_copy(cidx, ci_v, loc_sem.at[1]),
@@ -132,7 +162,7 @@
     ]
     for load in loads:
         load.start()
-    pl.semaphore_wait(barrier, len(peers))
+    pl.semaphore_wait(barrier, greeted)
 
     def cols(quarter, j):
         return pl.ds(pl.multiple_of(quarter * QUARTER + j * WIDTH, 128), WIDTH)
@@ -152,6 +182,17 @@
             same_quarter(ahead, k, g),
         )
 
+    def to_middle(k, j):
+        return remote(
+            pts.at[:, cols(quarter_at(k, g), j)], via.at[:, part(j)], yo_s.at[k, j], via_r.at[j],
+            device_of(middle, k, g),
+        )
+
+    def pass_on(j):
+        return remote(
+            via.at[:, part(j)], fb.at[onward, g, :, part(j)], via_s.at[j], f_r.at[onward, g, j], onward_to
+        )
+
     def sib_copy(i):
         quarter = pl.ds(pl.multiple_of(((quarter_at(1 - c, g) + i) % 4) * QUARTER, 128), QUARTER)
         return remote(pts.at[:, quarter], both.at[c, :, quarter], sib_s.at[i], sib_r.at[i], sibling)
@@ -165,7 +206,15 @@
     for j in range(CHUNKS):
         for k in (0, 1):
             x_copy(k, j).start()
-            yo_copy(k, j).start()
+
+            @pl.when(steps)
+            def _(k=k, j=j):
+                to_middle(k, j).start()
+
+            @pl.when(jnp.logical_not(steps))
+            def _(k=k, j=j):
+                yo_copy(k, j).start()
+
         sib_copy(j).start()
 
     loads[1].wait()
@@ -247,6 +296,12 @@
     gb_copy = remote(gb, gb_r, red_s.at[2], red_r.at[2], sibling)
 
     for j in range(CHUNKS):
+
+        @pl.when(passes)
+        def _(j=j):
+            to_middle(0, j).wait_recv()
+            pass_on(j).start()
+
         for way in (0, 1):
             remote(
                 pts.at[:, cols(0, 0)], xr.at[way, :, part(j)], x_s.at[0, j], x_r.at[way, j], sibling
@@ -387,6 +442,11 @@
             yo_copy(k, j).wait_send()
             relay(k, j).wait_send()
         sib_copy(j).wait_send()
+
+        @pl.when(passes)
+        def _(j=j):
+            pass_on(j).wait_send()
+
     for send in info_sends:
         send.wait_send()
     for copy in [gx_copy, gf_copy, rx_copy, rv_copy, *fu_copies, *sum_copies]:
@@ -447,6 +507,9 @@
         dma((10,)),
         dma((3,)),
         dma((3,)),
+        vmem((PTS, QUARTER), f32),
+        dma((CHUNKS,)),
+        dma((CHUNKS,)),
         dma((11,)),
         dma,
         dma,

time: 85.2 us -> 76.5 us (0.90)
  Pallas kernels: 79.8 us -> 71.4 us
    pallas_call x1, Pallas kernels: 79.8 us -> 71.4 us  [body(): pl.pallas_call(kernel, out_shape=jax.ShapeDtypeStruct((KNN, PTS), f32), i...]
where the time goes in v2:
time: 76.5 us; the launch traced here: 76.3 us
  Pallas kernels  71.4 us (93%)
  local copies, waits for them, and re-layouts  4.23 us (6%)
    pallas_call x1, Pallas kernels, body(): pl.pallas_call(kernel, out_shape=jax.ShapeDtypeStruct((KNN, PTS), f32), i...  71.4 us
    unnamed x9, local copies, waits for them, and re-layouts  4.23 us

profile of v2, /device:TPU:1, one launch (start us, length us, event | category | flops | bytes accessed | tf_op | source)
XLA Modules:
  0.0 76.3 jit_solution(14223803453320397121)
XLA Ops:
  0.7 0.0 copy-start
  0.7 1.6 %copy-done = f32[128,4096]{1,0:T(8,128)S(1)} copy-done((f32[128,4096]{1,0:T(8,128)S(1)}, f32[128,4096]{1,0:T(8,128)}, u32[]{:S(2)}) %copy-start) | copy-done | bytes 2097176
  2.2 0.0 copy-start.1
  2.2 0.7 copy-done.1
  2.9 0.0 copy-start.2
  2.9 0.7 copy-done.2
  3.6 0.0 copy-start.3
  3.6 0.7 copy-done.3
  4.3 71.4 %shard_map.55 = f32[16,128]{1,0:T(8,128)S(1)} custom-call(f32[128,4096]{1,0:T(8,128)S(1)} %copy-done, s32[1,128]{1,0:T(1,128)S(1)} %copy-done.3, s32[1]{0:T(128)S(6)} %copy.7.ccnt, s32[16,128]{1,0:T(8,128)S(1)} %bitcast.4, f32[16,128]{1,0:T(8,128)S(1)} %bitcast.5), custom_call_target="tpu_custom_call" | custom-call | tf_op jit(solution)/shard_map/pallas_call | solution.py:521
  75.7 0.6 copy.8
Async XLA Ops:
  0.7 1.6 %copy-start = (f32[128,4096]{1,0:T(8,128)S(1)}, f32[128,4096]{1,0:T(8,128)}, u32[]{:S(2)}) copy-start(f32[128,4096]{1,0:T(8,128)} %pts.1) | copy-start | bytes 6291460
  2.2 0.7 copy-start.1
  2.9 0.7 copy-start.2
  3.6 0.7 copy-start.3

commit v3 on v2

--- a/solution.py
+++ b/solution.py
@@ -123,13 +123,11 @@
         peers += row
     ring = q % 32
     steps = ((c == 1) & (ring == 31)) | ((c == 0) & (ring == 0))
-    passes = (ring == 28) | (ring == 3)
-    receives = (ring == 0) | (ring == 31)
-    onward = ring // 28
-    middle = q + 3 - 6 * c
-    source = device_of(q - 3 + 6 * onward, onward, g)
+    passes = (ring == 0) | (ring == 31)
+    onward = 1 - ring // 31
+    middle = q + 31 - 62 * c
+    source = device_of(q - 31 + 62 * onward, onward, g)
     after_node = (1 - d[0]) * 32 + 31 * (1 - onward)
-    before_node = (1 - d[0]) * 32 + jnp.where(ring == 0, 28, 3)
     onward_to = same_quarter(after_node, c, g)
 
     def greet(peer):
@@ -148,11 +146,7 @@
         greet(source)
         greet(onward_to)
 
-    @pl.when(receives)
-    def _():
-        greet(same_quarter(before_node, c, g))
-
-    greeted = len(peers) + jnp.where(steps, 2, 0) + jnp.where(passes, 2, 0) + jnp.where(receives, 1, 0)
+    greeted = len(peers) + jnp.where(steps, 2, 0) + jnp.where(passes, 2, 0)
     loads = [
         pltpu.make_async_copy(pts, both.at[c], loc_sem.at[0]),
         pltpu.make_async_copy(cidx, ci_v, loc_sem.at[1]),

time: 76.5 us -> 75.8 us (level)
  no operation moved by 1% of the time
where the time goes in v3:
time: 75.8 us; the launch traced here: 75.6 us
  Pallas kernels  70.7 us (93%)
  local copies, waits for them, and re-layouts  4.23 us (6%)
    pallas_call x1, Pallas kernels, body(): pl.pallas_call(kernel, out_shape=jax.ShapeDtypeStruct((KNN, PTS), f32), i...  70.7 us
    unnamed x9, local copies, waits for them, and re-layouts  4.23 us

profile of v3, /device:TPU:1, one launch (start us, length us, event | category | flops | bytes accessed | tf_op | source)
XLA Modules:
  0.0 75.6 jit_solution(13899159844938993874)
XLA Ops:
  0.7 0.0 copy-start
  0.7 1.6 %copy-done = f32[128,4096]{1,0:T(8,128)S(1)} copy-done((f32[128,4096]{1,0:T(8,128)S(1)}, f32[128,4096]{1,0:T(8,128)}, u32[]{:S(2)}) %copy-start) | copy-done | bytes 2097176
  2.2 0.0 copy-start.1
  2.2 0.7 copy-done.1
  2.9 0.0 copy-start.2
  2.9 0.7 copy-done.2
  3.6 0.0 copy-start.3
  3.6 0.7 copy-done.3
  4.3 70.7 %shard_map.55 = f32[16,128]{1,0:T(8,128)S(1)} custom-call(f32[128,4096]{1,0:T(8,128)S(1)} %copy-done, s32[1,128]{1,0:T(1,128)S(1)} %copy-done.3, s32[1]{0:T(128)S(6)} %copy.7.ccnt, s32[16,128]{1,0:T(8,128)S(1)} %bitcast.4, f32[16,128]{1,0:T(8,128)S(1)} %bitcast.5), custom_call_target="tpu_custom_call" | custom-call | tf_op jit(solution)/shard_map/pallas_call | solution.py:515
  75.0 0.6 copy.8
Async XLA Ops:
  0.7 1.6 %copy-start = (f32[128,4096]{1,0:T(8,128)S(1)}, f32[128,4096]{1,0:T(8,128)}, u32[]{:S(2)}) copy-start(f32[128,4096]{1,0:T(8,128)} %pts.1) | copy-start | bytes 6291460
  2.2 0.7 copy-start.1
  2.9 0.7 copy-start.2
  3.6 0.7 copy-start.3

commit v4 on v3

--- a/solution.py
+++ b/solution.py
@@ -17,8 +17,10 @@
 D = 4096
 KNN = 16
 QUARTER = 1024
-CHUNKS = 4
-WIDTH = QUARTER // CHUNKS
+WIDTHS = (256, 256, 256, 256)
+CHUNKS = len(WIDTHS)
+AHEAD = 3
+STARTS = tuple(sum(WIDTHS[:j]) for j in range(CHUNKS))
 FAR = 1e30
 DEAD = 1e35
 SUM_PHASES = ((3,), (0, 4, 2), (1,))
@@ -159,10 +161,10 @@
     pl.semaphore_wait(barrier, greeted)
 
     def cols(quarter, j):
-        return pl.ds(pl.multiple_of(quarter * QUARTER + j * WIDTH, 128), WIDTH)
+        return pl.ds(pl.multiple_of(quarter * QUARTER + STARTS[j], 128), WIDTHS[j])
 
     def part(j):
-        return pl.ds(j * WIDTH, WIDTH)
+        return pl.ds(STARTS[j], WIDTHS[j])
 
     def x_copy(k, j):
         return remote(
@@ -199,7 +201,8 @@
 
     for j in range(CHUNKS):
         for k in (0, 1):
-            x_copy(k, j).start()
+            if j < AHEAD:
+                x_copy(k, j).start()
 
             @pl.when(steps)
             def _(k=k, j=j):
@@ -209,7 +212,8 @@
             def _(k=k, j=j):
                 yo_copy(k, j).start()
 
-        sib_copy(j).start()
+    for i in range(4):
+        sib_copy(i).start()
 
     loads[1].wait()
     loads[4].wait()
@@ -271,12 +275,15 @@
                 remote(
                     xr.at[way, :, part(j)], fb.at[way, h, :, part(j)], yr_s.at[way, j], f_r.at[way, h, j], sibling
                 ).wait_recv()
-        v0 = near_blocks(0, j)
-        f = fb[1, :, :, part(j)].reshape(2 * PTS, WIDTH)
-        gf[0] += dot_nt(f, v0)
-        b = fb[0, :, :, part(j)].reshape(2 * PTS, WIDTH)
-        gb[...] += dot_nt(b, v0)
-        gf[1] += dot_nt(f, near_blocks(1, j))
+        f = fb[1, :, :, part(j)].reshape(2 * PTS, WIDTHS[j])
+        gf[1 - c] += dot_nt(f, near_blocks(1 - c, j))
+        if j == CHUNKS - 1:
+            gf_copy.start()
+        b = fb[0, :, :, part(j)].reshape(2 * PTS, WIDTHS[j])
+        gb[...] += dot_nt(b, near_blocks(0, j))
+        if j == CHUNKS - 1:
+            pl.when(c == 1)(gb_copy.start)
+        gf[c] += dot_nt(f, near_blocks(c, j))
 
     def far_quarter(j):
         sib_copy(j).wait_recv()
@@ -298,10 +305,15 @@
 
         for way in (0, 1):
             remote(
-                pts.at[:, cols(0, 0)], xr.at[way, :, part(j)], x_s.at[0, j], x_r.at[way, j], sibling
+                pts.at[:, cols(0, j)], xr.at[way, :, part(j)], x_s.at[0, j], x_r.at[way, j], sibling
             ).wait_recv()
             relay(way, j).start()
-        far_quarter(j)
+        if j + AHEAD < CHUNKS:
+            for k in (0, 1):
+                x_copy(k, j + AHEAD).start()
+        for i in range(4):
+            if i * CHUNKS // 4 == j:
+                far_quarter(i)
         xs = jnp.concatenate([xr[0, :, part(j)], xr[1, :, part(j)]], axis=0)
         own = jnp.concatenate([both[0, :, cols(mine_at, j)], both[1, :, cols(mine_at, j)]], axis=0)
         gx[...] += dot_nt(xs, own)
@@ -325,12 +337,6 @@
 
     lax.fori_loop(1, 10, each, 0)
     far_products(CHUNKS - 1)
-    gf_copy.start()
-
-    @pl.when(c == 1)
-    def _():
-        gb_copy.start()
-
     gf_copy.wait_recv()
     total = gf[c] + gf_r[...]
     for rel in (0, 1):
@@ -435,12 +441,13 @@
             x_copy(k, j).wait_send()
             yo_copy(k, j).wait_send()
             relay(k, j).wait_send()
-        sib_copy(j).wait_send()
 
         @pl.when(passes)
         def _(j=j):
             pass_on(j).wait_send()
 
+    for i in range(4):
+        sib_copy(i).wait_send()
     for send in info_sends:
         send.wait_send()
     for copy in [gx_copy, gf_copy, rx_copy, rv_copy, *fu_copies, *sum_copies]:

time: 75.8 us -> 73.8 us (0.974)
  Pallas kernels: 70.7 us -> 68.7 us
    pallas_call x1, Pallas kernels: 70.7 us -> 68.7 us  [body(): pl.pallas_call(kernel, out_shape=jax.ShapeDtypeStruct((KNN, PTS), f32), i...]
where the time goes in v4:
time: 73.8 us; the launch traced here: 73.6 us
  Pallas kernels  68.7 us (93%)
  local copies, waits for them, and re-layouts  4.23 us (6%)
    pallas_call x1, Pallas kernels, body(): pl.pallas_call(kernel, out_shape=jax.ShapeDtypeStruct((KNN, PTS), f32), i...  68.7 us
    unnamed x9, local copies, waits for them, and re-layouts  4.23 us

profile of v4, /device:TPU:1, one launch (start us, length us, event | category | flops | bytes accessed | tf_op | source)
XLA Modules:
  0.0 73.6 jit_solution(15224296580705211207)
XLA Ops:
  0.7 0.0 copy-start
  0.7 1.6 %copy-done = f32[128,4096]{1,0:T(8,128)S(1)} copy-done((f32[128,4096]{1,0:T(8,128)S(1)}, f32[128,4096]{1,0:T(8,128)}, u32[]{:S(2)}) %copy-start) | copy-done | bytes 2097176
  2.2 0.0 copy-start.1
  2.2 0.7 copy-done.1
  2.9 0.0 copy-start.2
  2.9 0.7 copy-done.2
  3.6 0.0 copy-start.3
  3.6 0.7 copy-done.3
  4.3 68.7 %shard_map.55 = f32[16,128]{1,0:T(8,128)S(1)} custom-call(f32[128,4096]{1,0:T(8,128)S(1)} %copy-done, s32[1,128]{1,0:T(1,128)S(1)} %copy-done.3, s32[1]{0:T(128)S(6)} %copy.7.ccnt, s32[16,128]{1,0:T(8,128)S(1)} %bitcast.4, f32[16,128]{1,0:T(8,128)S(1)} %bitcast.5), custom_call_target="tpu_custom_call" | custom-call | tf_op jit(solution)/shard_map/pallas_call | solution.py:522
  73.0 0.6 copy.8
Async XLA Ops:
  0.7 1.6 %copy-start = (f32[128,4096]{1,0:T(8,128)S(1)}, f32[128,4096]{1,0:T(8,128)}, u32[]{:S(2)}) copy-start(f32[128,4096]{1,0:T(8,128)} %pts.1) | copy-start | bytes 6291460
  2.2 0.7 copy-start.1
  2.9 0.7 copy-start.2
  3.6 0.7 copy-start.3

commit v5 on v4

--- a/solution.py
+++ b/solution.py
@@ -199,19 +199,20 @@
             xr.at[way, :, part(j)], fb.at[way, 1 - g, :, part(j)], yr_s.at[way, j], f_r.at[way, 1 - g, j], to
         )
 
+    def yo_start(k, j):
+        @pl.when(steps)
+        def _():
+            to_middle(k, j).start()
+
+        @pl.when(jnp.logical_not(steps))
+        def _():
+            yo_copy(k, j).start()
+
     for j in range(CHUNKS):
         for k in (0, 1):
             if j < AHEAD:
                 x_copy(k, j).start()
-
-            @pl.when(steps)
-            def _(k=k, j=j):
-                to_middle(k, j).start()
-
-            @pl.when(jnp.logical_not(steps))
-            def _(k=k, j=j):
-                yo_copy(k, j).start()
-
+                yo_start(k, j)
     for i in range(4):
         sib_copy(i).start()
 
@@ -311,12 +312,20 @@
         if j + AHEAD < CHUNKS:
             for k in (0, 1):
                 x_copy(k, j + AHEAD).start()
+                yo_start(k, j + AHEAD)
         for i in range(4):
-            if i * CHUNKS // 4 == j:
+            if max(i - 1, 0) == j:
                 far_quarter(i)
         xs = jnp.concatenate([xr[0, :, part(j)], xr[1, :, part(j)]], axis=0)
         own = jnp.concatenate([both[0, :, cols(mine_at, j)], both[1, :, cols(mine_at, j)]], axis=0)
         gx[...] += dot_nt(xs, own)
+        if j == CHUNKS - 2:
+            def each(s, carry):
+                remote(info.at[0], info.at[s], info_s.at[0], info_r.at[s], sibling).wait_recv()
+                set_bias(s)
+                return carry
+
+            lax.fori_loop(1, 10, each, 0)
         if j == CHUNKS - 1:
             gx_copy.start()
         if j > 0:
@@ -330,12 +339,6 @@
     rx_copy = remote(hx.at[c], rx, t_s.at[0], rx_sem, other)
     rx_copy.start()
 
-    def each(s, carry):
-        remote(info.at[0], info.at[s], info_s.at[0], info_r.at[s], sibling).wait_recv()
-        set_bias(s)
-        return carry
-
-    lax.fori_loop(1, 10, each, 0)
     far_products(CHUNKS - 1)
     gf_copy.wait_recv()
     total = gf[c] + gf_r[...]

time: 73.8 us -> 73.3 us (level)
  no operation moved by 1% of the time
where the time goes in v5:
time: 73.3 us; the launch traced here: 73.1 us
  Pallas kernels  68.2 us (93%)
  local copies, waits for them, and re-layouts  4.23 us (6%)
    pallas_call x1, Pallas kernels, body(): pl.pallas_call(kernel, out_shape=jax.ShapeDtypeStruct((KNN, PTS), f32), i...  68.2 us
    unnamed x9, local copies, waits for them, and re-layouts  4.23 us

profile of v5, /device:TPU:1, one launch (start us, length us, event | category | flops | bytes accessed | tf_op | source)
XLA Modules:
  0.0 73.1 jit_solution(7304359173339738555)
XLA Ops:
  0.7 0.0 copy-start
  0.7 1.6 %copy-done = f32[128,4096]{1,0:T(8,128)S(1)} copy-done((f32[128,4096]{1,0:T(8,128)S(1)}, f32[128,4096]{1,0:T(8,128)}, u32[]{:S(2)}) %copy-start) | copy-done | bytes 2097176
  2.2 0.0 copy-start.1
  2.2 0.7 copy-done.1
  2.9 0.0 copy-start.2
  2.9 0.7 copy-done.2
  3.6 0.0 copy-start.3
  3.6 0.7 copy-done.3
  4.3 68.2 %shard_map.55 = f32[16,128]{1,0:T(8,128)S(1)} custom-call(f32[128,4096]{1,0:T(8,128)S(1)} %copy-done, s32[1,128]{1,0:T(1,128)S(1)} %copy-done.3, s32[1]{0:T(128)S(6)} %copy.7.ccnt, s32[16,128]{1,0:T(8,128)S(1)} %bitcast.4, f32[16,128]{1,0:T(8,128)S(1)} %bitcast.5), custom_call_target="tpu_custom_call" | custom-call | tf_op jit(solution)/shard_map/pallas_call | solution.py:525
  72.5 0.6 copy.8
Async XLA Ops:
  0.7 1.6 %copy-start = (f32[128,4096]{1,0:T(8,128)S(1)}, f32[128,4096]{1,0:T(8,128)}, u32[]{:S(2)}) copy-start(f32[128,4096]{1,0:T(8,128)} %pts.1) | copy-start | bytes 6291460
  2.2 0.7 copy-start.1
  2.9 0.7 copy-start.2
  3.6 0.7 copy-start.3

commit v6 on v5

--- a/solution.py
+++ b/solution.py
@@ -350,17 +350,21 @@
     def ru_copy(src, half_slot, rel, h, sem, to):
         name = g if rel == 0 else 1 - g
         return remote(
-            src.at[rel, pl.ds(h * PTS, PTS)], ru.at[g, half_slot, name], sem, ru_sem.at[g, half_slot, name], to
+            src.at[rel, pl.ds(pl.multiple_of(h * PTS, PTS), PTS)], ru.at[g, half_slot, name], sem, ru_sem.at[g, half_slot, name], to
         )
 
     fu_copies = [
-        ru_copy(hf, c, rel, h, t_s.at[2 + 2 * rel + h], device_of(down, 1, h)) for rel in (0, 1) for h in (0, 1)
+        ru_copy(hf, c, rel, h, t_s.at[2 + rel + 2 * i], device_of(down, 1, h))
+        for i, h in enumerate((1 - g, g))
+        for rel in (0, 1)
     ]
     for copy in fu_copies:
         copy.start()
     rbv_copy = remote(hb.at[1], rbv, t_s.at[6], rbv_sem, device_of(q, 0, 1 - g))
     bu_copies = [
-        ru_copy(hb, 1, rel, h, t_s.at[7 + 2 * rel + h], device_of(up, 0, h)) for rel in (0, 1) for h in (0, 1)
+        ru_copy(hb, 1, rel, h, t_s.at[7 + rel + 2 * i], device_of(up, 0, h))
+        for i, h in enumerate((1 - g, g))
+        for rel in (0, 1)
     ]
 
     @pl.when(c == 0)

time: 73.3 us -> 73.3 us (level)
  no operation moved by 1% of the time
where the time goes in v6:
time: 73.3 us; the launch traced here: 73.1 us
  Pallas kernels  68.2 us (93%)
  local copies, waits for them, and re-layouts  4.23 us (6%)
    pallas_call x1, Pallas kernels, body(): pl.pallas_call(kernel, out_shape=jax.ShapeDtypeStruct((KNN, PTS), f32), i...  68.2 us
    unnamed x9, local copies, waits for them, and re-layouts  4.23 us

profile of v6, /device:TPU:1, one launch (start us, length us, event | category | flops | bytes accessed | tf_op | source)
XLA Modules:
  0.0 73.1 jit_solution(13437039074344959612)
XLA Ops:
  0.7 0.0 copy-start
  0.7 1.6 %copy-done = f32[128,4096]{1,0:T(8,128)S(1)} copy-done((f32[128,4096]{1,0:T(8,128)S(1)}, f32[128,4096]{1,0:T(8,128)}, u32[]{:S(2)}) %copy-start) | copy-done | bytes 2097176
  2.2 0.0 copy-start.1
  2.2 0.7 copy-done.1
  2.9 0.0 copy-start.2
  2.9 0.7 copy-done.2
  3.6 0.0 copy-start.3
  3.6 0.7 copy-done.3
  4.3 68.2 %shard_map.55 = f32[16,128]{1,0:T(8,128)S(1)} custom-call(f32[128,4096]{1,0:T(8,128)S(1)} %copy-done, s32[1,128]{1,0:T(1,128)S(1)} %copy-done.3, s32[1]{0:T(128)S(6)} %copy.7.ccnt, s32[16,128]{1,0:T(8,128)S(1)} %bitcast.4, f32[16,128]{1,0:T(8,128)S(1)} %bitcast.5), custom_call_target="tpu_custom_call" | custom-call | tf_op jit(solution)/shard_map/pallas_call | solution.py:529
  72.5 0.6 copy.8
Async XLA Ops:
  0.7 1.6 %copy-start = (f32[128,4096]{1,0:T(8,128)S(1)}, f32[128,4096]{1,0:T(8,128)}, u32[]{:S(2)}) copy-start(f32[128,4096]{1,0:T(8,128)} %pts.1) | copy-start | bytes 6291460
  2.2 0.7 copy-start.1
  2.9 0.7 copy-start.2
  3.6 0.7 copy-start.3
